TPU v7x, 128 devices: a whole 4x4x4 slice. The times are simulated.
128 devices in a mesh: tm: 4 (over x), op: 32 (over y, z, core).
Axes of the slice: x: 4, y: 4, z: 4, core: 2. Of those that a mesh axis runs over, the one named last changes fastest.
Arguments:
- sink_elem: bfloat16 [2, 4, 2048, 16384], P(None, 'tm', 'op'), may hold values from -6 to 6
- source_elem: bfloat16 [2, 2, 2048, 16384], P(None, None, None, 'op'), may hold values from -6 to 6
- peram: bfloat16 [2, 4, 2, 512, 512], P(None, 'tm', None, 'op'), may hold values from -4 to 4
- pair_list: int32 [16, 1], replicated, may hold values from 0 to 15
- spin_sets: int32 [16, 3], replicated, may hold values from 0 to 3
Outputs:
- correlator: float32 [2, 4, 2, 16, 1], P(None, 'tm')
All inputs are finite; a program needn't handle non-finite values.
Results may differ from a plain program's by a relative error of at most 0.0041.
Values may be sent and summed in bfloat16 or wider, within the bound.
A program may use at most 192 MiB of HBM per device.

v0:
```python
import jax
import jax.numpy as jnp
from jax import lax
from jax.sharding import PartitionSpec as P

NEV = 128
NSPIN = 4
NOP = 16
TSRC = 2
PAIRS = 1


def complex_matrix(block):
    upper = jnp.concatenate([block[0], block[1]], axis=1)
    lower = jnp.concatenate([-block[1], block[0]], axis=1)
    return jnp.stack([upper, lower])


def on_device(sink_elem, source_elem, peram, pair_list, spin_sets):
    tau_all = lax.all_gather(peram, "op", axis=3, tiled=True)
    position = lax.axis_index("op")
    rows = sink_elem.shape[2]
    local_times = sink_elem.shape[1]
    span = min(rows, NEV)
    cols = source_elem.shape[3]

    def spin_block(local, t0, left, right):
        return lax.dynamic_slice(tau_all[:, local, t0], (0, left * NEV, right * NEV), (2, NEV, NEV))

    def sink_side(local, t0, p):
        op_now = (position * rows + 0) // NEV
        mine = spin_sets[op_now]
        theirs = spin_sets[pair_list[op_now, p]]
        third = complex_matrix(spin_block(local, t0, mine[2], theirs[2]))
        second = complex_matrix(spin_block(local, t0, mine[1], theirs[1]))
        phi = sink_elem[:, local, 0:span].reshape(2, span * NEV, NEV)
        x_both = jnp.einsum("cxk,ckb->xb", phi, third, preferred_element_type=jnp.float32)
        x_both = x_both.astype(jnp.bfloat16).reshape(span, NEV, 2, NEV)
        y_both = jnp.einsum("ijck,cjb->ibk", x_both, second, preferred_element_type=jnp.float32)
        y_both = y_both.astype(jnp.bfloat16).reshape(span, 2, NEV * NEV)
        pieces = jnp.transpose(y_both, (1, 0, 2))
        return pieces

    partial_terms = {}
    combos = [
        (local, t0, p) for local in range(local_times) for t0 in range(TSRC) for p in range(PAIRS)
    ]
    stacked = jnp.stack([sink_side(local, t0, p) for local, t0, p in combos], axis=1)
    columns = lax.all_to_all(stacked, "op", split_axis=3, concat_axis=2, tiled=True)
    for index, combo in enumerate(combos):
        column_t0 = combo[1]
        other = pair_list[:, combo[2]]
        source = source_elem[:, column_t0].reshape(2, NOP, NEV, cols)
        chosen = jnp.take(source, other, axis=1)
        tiles = columns[:, index].reshape(2, NOP, NEV, cols)

        def inner(a, b):
            return jnp.einsum("oic,ojc->oij", a, b, preferred_element_type=jnp.float32)

        m_re = inner(tiles[0], chosen[0]) + inner(tiles[1], chosen[1])
        m_im = inner(tiles[1], chosen[0]) - inner(tiles[0], chosen[1])
        blocks = tau_all[:, combo[0], column_t0].reshape(2, NSPIN, NEV, NSPIN, NEV)
        blocks = jnp.transpose(blocks, (1, 3, 0, 2, 4))
        first = blocks[spin_sets[:, 0], spin_sets[other, 0]].astype(jnp.float32)
        c_re = jnp.sum(first[:, 0] * m_re - first[:, 1] * m_im, axis=(1, 2))
        c_im = jnp.sum(first[:, 0] * m_im + first[:, 1] * m_re, axis=(1, 2))
        partial_terms[combo] = jnp.stack([c_re, c_im])
    local = 0
    per_time = []
    for t0 in range(TSRC):
        per_time.append(jnp.stack([partial_terms[local, t0, 0]], axis=-1))
    per_local = [jnp.stack(per_time, axis=1)]
    partial_sum = jnp.stack(per_local, axis=1)
    totals = lax.psum(partial_sum, "op")
    return totals * (1.0 / float(NEV**3))


def solution(mesh):
    in_specs = (
        P(None, "tm", "op", None),
        P(None, None, None, "op"),
        P(None, "tm", None, "op", None),
        P(),
        P(),
    )
    out_specs = P(None, "tm", None, None, None)
    return jax.shard_map(
        on_device, mesh=mesh, in_specs=in_specs, out_specs=out_specs, check_vma=False
    )
```

profile of v0, /device:TPU:1, one launch (start us, length us, event | category | flops | bytes accessed | tf_op | source)
XLA Modules:
  0.0 462.1 jit_solution(5356037397111504323)
XLA Ops:
  6.5 1.5 copy.40
  8.1 1.2 constant_dynamic-slice_fusion.1
  11.3 0.8 constant_dynamic-slice_fusion
  15.2 7.4 %reshape_squeeze.19 = bf16[2,8192,128]{2,1,0:T(8,128)(2,1)} reshape(bf16[2,1,64,16384]{3,2,1,0:T(8,128)(2,1)} %param.7) | data formatting | bytes 8388608 | tf_op jit(solution)/shard_map/reshape;squeeze | solution.py:36
  22.6 34.7 %all-gather.2.cloned.1.call-done = bf16[2,1,2,512,512]{4,2,1,0,3:T(2,128)(2,1)} async-done(((bf16[2,1,2,16,512]{4,2,1,0,3:T(2,128)(2,1)}), bf16[2,1,2,512,512]{4,2,1,0,3:T(2,128)(2,1)}) %all-gather.2.cloned.1.call-update) | async-done | bytes 2097168 | tf_op jit(solution)/shard_map/all_gather | solution.py:20
  57.3 6.5 %fusion.57 = (bf16[2,1,1,512,512]{4,2,1,0,3:T(2,128)(2,1)}, bf16[2,1,1,512,512]{4,2,1,0,3:T(2,128)(2,1)S(1)}) fusion(bf16[2,1,2,512,512]{4,2,1,0,3:T(2,128)(2,1)} %all-gather.2.cloned.1.call-done), kind=kLoop, calls=%fused_computation.113 | loop fusion | bytes 4194304 | tf_op jit(solution)/shard_map/slice | solution.py:62
  63.8 4.6 copy.59
  68.4 4.2 copy.60
  72.6 0.8 dynamic-slice_bitcast_fusion.3
  73.4 0.8 fusion.53
  74.2 3.5 fusion.15
  77.7 1.2 copy.61
  78.9 7.4 %fusion.2 = bf16[64,256,128]{2,1,0:T(8,128)(2,1)} fusion(bf16[64,128,2,128]{1,0,3,2:T(8,128)(2,1)S(1)} %bitcast.218, bf16[1,128,256]{1,2,0:T(8,128)(2,1)S(1)} %get-tuple-element.35, bf16[1,128,256]{1,2,0:T(8,128)(2,1)S(1)} %get-tuple-element.34), kind=kOutput, calls=%fused_computation.12 | convolution fusion | flops 1076101120 | bytes 8519680 | tf_op jit(solution)/shard_map/ijck,cjb->ibk/dot_general | solution.py:39
  86.4 6.9 %reshape.75 = bf16[64,2,16384]{2,1,0:T(2,128)(2,1)} reshape(bf16[64,256,128]{2,1,0:T(8,128)(2,1)} %fusion.2) | data formatting | bytes 8388608 | tf_op jit(solution)/shard_map/reshape | solution.py:40
  93.2 6.6 %copy.83 = bf16[64,2,16384]{2,0,1:T(8,128)(2,1)} copy(bf16[64,2,16384]{2,1,0:T(2,128)(2,1)} %reshape.75) | data formatting | bytes 8388608 | tf_op jit(solution)/shard_map/reshape | solution.py:40
  99.9 1.3 fusion.14
  101.2 1.2 copy.62
  102.4 7.4 %fusion.3 = bf16[64,256,128]{2,1,0:T(8,128)(2,1)} fusion(bf16[64,128,2,128]{1,0,3,2:T(8,128)(2,1)S(1)} %bitcast.219, bf16[1,128,256]{1,2,0:T(8,128)(2,1)S(1)} %get-tuple-element.39, bf16[1,128,256]{1,2,0:T(8,128)(2,1)S(1)} %get-tuple-element.38), kind=kOutput, calls=%fused_computation.13 | convolution fusion | flops 1076101120 | bytes 8519680 | tf_op jit(solution)/shard_map/ijck,cjb->ibk/dot_general | solution.py:39
  109.8 6.9 %reshape.77 = bf16[64,2,16384]{2,1,0:T(2,128)(2,1)} reshape(bf16[64,256,128]{2,1,0:T(8,128)(2,1)} %fusion.3) | data formatting | bytes 8388608 | tf_op jit(solution)/shard_map/reshape | solution.py:40
  116.7 6.6 %copy.82 = bf16[64,2,16384]{2,0,1:T(8,128)(2,1)} copy(bf16[64,2,16384]{2,1,0:T(2,128)(2,1)} %reshape.77) | data formatting | bytes 8388608 | tf_op jit(solution)/shard_map/reshape | solution.py:40
  123.3 6.2 %pad_maximum_fusion = bf16[2,2,64,16384]{3,2,1,0:T(8,128)(2,1)} fusion(bf16[2,1,64,16384]{3,2,1,0:T(8,128)(2,1)} %bitcast.222, bf16[2,1,64,16384]{3,2,1,0:T(8,128)(2,1)S(1)} %bitcast.220), kind=kLoop, calls=%fused_computation.9 | loop fusion | flops 4194304 | bytes 16777216 | tf_op jit(solution)/shard_map/stack | solution.py:48
  129.5 34.5 %copy.49 = bf16[2,2,64,16384]{2,1,0,3:T(2,128)(2,1)} copy(bf16[2,2,64,16384]{3,2,1,0:T(8,128)(2,1)} %pad_maximum_fusion) | data formatting | bytes 16777216 | tf_op jit(solution)/shard_map/stack | solution.py:48
  164.0 26.7 %reshape.124 = bf16[32,2,65536]{2,1,0:T(2,128)(2,1)} reshape(bf16[16384,2,2,64]{3,2,1,0:T(2,128)(2,1)} %bitcast.211) | data formatting | bytes 16777216
  190.7 5.4 %all-to-all-start = ((bf16[32,2,65536]{2,1,0:T(2,128)(2,1)}), bf16[32,2,65536]{2,1,0:T(2,128)(2,1)}, u32[]{:S(2)}, u32[]{:S(2)}) async-start(bf16[32,2,65536]{2,1,0:T(2,128)(2,1)} %reshape.124), calls=%async_computation | async-start | bytes 16777216 | tf_op jit(solution)/shard_map/all_to_all | solution.py:49
  196.2 5.8 %fusion.56 = (bf16[2,1,2048,512]{3,2,1,0:T(8,128)(2,1)}, bf16[2,1,2048,512]{3,2,1,0:T(8,128)(2,1)}) fusion(bf16[2,2,2048,512]{3,2,1,0:T(8,128)(2,1)} %param.8), kind=kLoop, calls=%fused_computation.112 | loop fusion | bytes 16777216 | tf_op jit(solution)/shard_map/slice | solution.py:53
  202.0 5.0 %gather_fusion.3 = bf16[16,2,128,512]{3,2,1,0:T(8,128)(2,1)} fusion(bf16[2,16,128,512]{3,2,1,0:T(8,128)(2,1)} %bitcast.223, s32[1024]{0:T(1024)S(1)} %pad_clamp_fusion), kind=kCustom, calls=%fused_computation.clone | custom fusion | bytes 8388672 | tf_op jit(solution)/shard_map/jit(_take)/gather | solution.py:54
  207.0 5.0 %gather_fusion.4 = bf16[16,2,128,512]{3,2,1,0:T(8,128)(2,1)} fusion(bf16[2,16,128,512]{3,2,1,0:T(8,128)(2,1)} %bitcast.221, s32[1024]{0:T(1024)S(1)} %pad_clamp_fusion), kind=kCustom, calls=%fused_computation.1.clone | custom fusion | bytes 8388672 | tf_op jit(solution)/shard_map/jit(_take)/gather | solution.py:54
  212.7 6.0 %fusion.5 = (bf16[2,16,128,512]{3,2,1,0:T(8,128)(2,1)}, bf16[2,16,128,512]{3,2,1,0:T(8,128)(2,1)}) fusion(bf16[16,2,128,512]{3,2,1,0:T(8,128)(2,1)} %gather_fusion.3, pred[16]{0:T(512)(128)(4,1)S(1)} %compare_and_fusion, bf16[16,2,128,512]{3,2,1,0:T(8,128)(2,1)} %gather_fusion.4), kind=kLoop, calls=%fused_computation.17 | loop fusion | flops 4194304 | bytes 16777232 | tf_op jit(solution)/shard_map/jit(_take)/select_n | solution.py:54
  218.9 1.1 reshape_squeeze.21
  220.1 1.5 copy.42
  221.6 1.7 copy.52
  223.3 2.0 gather_fusion.1
  225.3 0.8 gather_fusion.2
  226.0 1.5 copy_convert_fusion.1
  227.6 1.6 copy_convert_fusion
  229.2 75.5 %all-to-all-done = bf16[32,2,65536]{2,1,0:T(2,128)(2,1)} async-done(((bf16[32,2,65536]{2,1,0:T(2,128)(2,1)}), bf16[32,2,65536]{2,1,0:T(2,128)(2,1)}, u32[]{:S(2)}, u32[]{:S(2)}) %all-to-all-start) | async-done | bytes 8388640 | tf_op jit(solution)/shard_map/all_to_all | solution.py:49
  304.7 26.0 %reshape.125 = bf16[16384,2,2,64]{3,2,1,0:T(2,128)(2,1)} reshape(bf16[32,2,65536]{2,1,0:T(2,128)(2,1)} %all-to-all-done) | data formatting | bytes 16777216
  330.7 36.1 %copy.50 = bf16[2,2,32,64,512]{4,3,2,1,0:T(8,128)(2,1)} copy(bf16[2,2,32,64,512]{3,1,0,4,2:T(2,128)(2,1)} %bitcast.212) | data formatting | bytes 16777216 | tf_op jit(solution)/shard_map/all_to_all | solution.py:49
  366.8 4.0 fusion.55
  372.1 0.7 fusion.16
  372.9 0.8 fusion.26
  373.6 1.4 copy-done.2
  376.5 0.7 fusion.24
  377.2 0.9 copy-done.7
  378.0 0.8 subtract_reduce_fusion.1
  378.9 0.7 copy-done.6
  379.6 0.8 subtract_reduce_fusion
  380.5 74.2 %psum.7 = f32[2,1,2,16,1]{3,2,0,4,1:T(2,128)S(1)} all-reduce(f32[2,1,2,16,1]{3,2,0,4,1:T(2,128)S(1)} %bitcast.230), channel_id=1, replica_groups=mesh['tm'=4,'op'=32] {'op'}, use_global_device_ids=true, to_apply=%region_4.6 | all-reduce | flops 64 | bytes 512 | tf_op jit(solution)/shard_map/psum | solution.py:74
  (39 shorter events, 5.1 us)
Async XLA Ops:
  6.5 50.8 %all-gather.2.cloned.1.call-start = ((), (), s32[]{:S(2)}) async-start(), calls=%async_computation.1 | async-start | bytes 2162688 | tf_op jit(solution)/shard_map/all_gather | solution.py:20
  93.2 6.6 %copy-start.1 = (bf16[2,8192,128]{2,1,0:T(8,128)(2,1)S(1)}, bf16[2,8192,128]{2,1,0:T(8,128)(2,1)}, u32[]{:S(2)}) copy-start(bf16[2,8192,128]{2,1,0:T(8,128)(2,1)} %reshape_squeeze.19) | copy-start | bytes 12582916
  116.7 6.6 %copy-start.4 = (bf16[64,2,16384]{2,0,1:T(8,128)(2,1)S(1)}, bf16[64,2,16384]{2,0,1:T(8,128)(2,1)}, u32[]{:S(2)}) copy-start(bf16[64,2,16384]{2,0,1:T(8,128)(2,1)} %copy.83) | copy-start | bytes 12582916
  190.7 5.4 %copy-start.8 = (s32[16,1]{0,1:T(1,128)S(1)}, s32[16,1]{0,1:T(1,128)}, u32[]{:S(2)}) copy-start(s32[16,1]{0,1:T(1,128)} %param.10) | copy-start | bytes 196
  190.7 114.0 %all-to-all-start = ((bf16[32,2,65536]{2,1,0:T(2,128)(2,1)}), bf16[32,2,65536]{2,1,0:T(2,128)(2,1)}, u32[]{:S(2)}, u32[]{:S(2)}) async-start(bf16[32,2,65536]{2,1,0:T(2,128)(2,1)} %reshape.124), calls=%async_computation | async-start | bytes 16777216 | tf_op jit(solution)/shard_map/all_to_all | solution.py:49
  207.0 5.0 %copy-start = (s32[16,3]{0,1:T(4,128)S(1)}, s32[16,3]{0,1:T(4,128)}, u32[]{:S(2)}) copy-start(s32[16,3]{0,1:T(4,128)} %param.11) | copy-start | bytes 580
  212.7 6.3 %copy-start.5 = (bf16[2,1,1,512,512]{3,4,2,1,0:T(8,128)(2,1)S(1)}, bf16[2,1,1,512,512]{3,4,2,1,0:T(8,128)(2,1)}, u32[]{:S(2)}) copy-start(bf16[2,1,1,512,512]{3,4,2,1,0:T(8,128)(2,1)} %copy.60) | copy-start | bytes 3145732
  366.8 4.7 %copy-start.3 = (bf16[2,16,128,512]{3,2,1,0:T(8,128)(2,1)S(1)}, bf16[2,16,128,512]{3,2,1,0:T(8,128)(2,1)}, u32[]{:S(2)}) copy-start(bf16[2,16,128,512]{3,2,1,0:T(8,128)(2,1)} %get-tuple-element.48) | copy-start | bytes 12582916
  372.8 2.2 copy-start.2
  376.5 1.6 copy-start.7
  378.0 1.6 copy-start.6
Sparse Core Ops, SparseCore 0:
  9.6 47.6 all-gather.1
where the time goes:
time: 467 us; the launch traced here: 462 us
  local copies, waits for them, and re-layouts  212 us (45%)
  waiting for transfers between devices  110 us (24%)
  blocking collectives  74.2 us (16%)
  matrix products  25.6 us (5%)
  between operations  18.1 us (4%)
  other arithmetic  16.8 us (4%)
  starting transfers between devices  5.43 us (1%)
    all_to_all x1, waiting for transfers between devices, on_device(): lax.all_to_all(stacked, 'op', split_axis=3, concat_axis=2, tiled=True)  75.5 us
    psum x1, blocking collectives, on_device(): totals = lax.psum(partial_sum, 'op')  74.2 us
    unnamed x25, local copies, waits for them, and re-layouts  69.1 us
    all_to_all x1, local copies, waits for them, and re-layouts, on_device(): lax.all_to_all(stacked, 'op', split_axis=3, concat_axis=2, tiled=True)  36.1 us
    all_gather x1, waiting for transfers between devices, on_device(): tau_all = lax.all_gather(peram, 'op', axis=3, tiled=True)  34.7 us
    another operation x1, local copies, waits for them, and re-layouts, on_device(): jnp.stack([sink_side(local, t0, p) for local, t0, p in combos], axis=1)  34.5 us
    reshape x4, local copies, waits for them, and re-layouts, sink_side(): y_both = y_both.astype(jnp.bfloat16).reshape(span, 2, NEV * NEV)  27 us
    dot_general x2, matrix products, sink_side(): jnp.einsum('ijck,cjb->ibk', x_both, second, preferred_element_type=jnp.fl...  14.9 us
  transfers between devices with their start and end apart: 2, of which 2 were waited for; matrix products, arithmetic and copies ran while one was open for 9% of the time, Pallas kernels for 0%

commit v1 on v0

--- a/solution.py
+++ b/solution.py
@@ -71,7 +71,16 @@
         per_time.append(jnp.stack([partial_terms[local, t0, 0]], axis=-1))
     per_local = [jnp.stack(per_time, axis=1)]
     partial_sum = jnp.stack(per_local, axis=1)
-    totals = lax.psum(partial_sum, "op")
+
+    def write_routes_all_over_axis(own_rows, shard_axis):
+        k_all = lax.axis_size(shard_axis)
+        y1 = lambda k_now: [(src_i, src_i ^ k_now) for src_i in range(k_all)]
+        far_arr = own_rows
+        for idx in range(k_all.bit_length() - 1):
+            far_arr = far_arr + lax.ppermute(far_arr, axis_name=shard_axis, perm=y1(1 << idx))
+        return far_arr
+
+    totals = write_routes_all_over_axis(partial_sum, "op")
     return totals * (1.0 / float(NEV**3))
 
 

time: 467 us -> 426 us (0.912)
  blocking collectives: 74.2 us -> 0 us
  starting transfers between devices: 5.43 us -> 27 us
  waiting for transfers between devices: 110 us -> 118 us
    psum x1 -> x0, blocking collectives: 74.2 us -> none  [on_device(): totals = lax.psum(partial_sum, 'op')]
    ppermute x0 -> x5, starting transfers between devices: none -> 21.6 us  [write_routes_all_over_axis(): lax.ppermute(far_arr, axis_name=shard_axis, perm=y1(1 << idx))]
    ppermute x0 -> x5, waiting for transfers between devices: none -> 9.59 us  [write_routes_all_over_axis(): lax.ppermute(far_arr, axis_name=shard_axis, perm=y1(1 << idx))]
  transfers between devices with their start and end apart: 2 -> 7, of which waited for: 2 -> 7; matrix products, arithmetic and copies ran while one was open for 9% -> 10% of each run, Pallas kernels for 0% -> 0%
where the time goes in v1:
time: 426 us; the launch traced here: 418 us
  local copies, waits for them, and re-layouts  212 us (50%)
  waiting for transfers between devices  118 us (28%)
  starting transfers between devices  27 us (6%)
  matrix products  25.6 us (6%)
  between operations  18.2 us (4%)
  other arithmetic  17 us (4%)
    all_to_all x1, waiting for transfers between devices, on_device(): lax.all_to_all(stacked, 'op', split_axis=3, concat_axis=2, tiled=True)  74 us
    unnamed x25, local copies, waits for them, and re-layouts  69.1 us
    all_to_all x1, local copies, waits for them, and re-layouts, on_device(): lax.all_to_all(stacked, 'op', split_axis=3, concat_axis=2, tiled=True)  36 us
    all_gather x1, waiting for transfers between devices, on_device(): tau_all = lax.all_gather(peram, 'op', axis=3, tiled=True)  34.6 us
    another operation x1, local copies, waits for them, and re-layouts, on_device(): jnp.stack([sink_side(local, t0, p) for local, t0, p in combos], axis=1)  34.5 us
    reshape x4, local copies, waits for them, and re-layouts, sink_side(): y_both = y_both.astype(jnp.bfloat16).reshape(span, 2, NEV * NEV)  27 us
    ppermute x5, starting transfers between devices, write_routes_all_over_axis(): lax.ppermute(far_arr, axis_name=shard_axis, perm=y1(1 << idx))  21.6 us
    dot_general x2, matrix products, sink_side(): jnp.einsum('ijck,cjb->ibk', x_both, second, preferred_element_type=jnp.fl...  14.9 us
  transfers between devices with their start and end apart: 7, of which 7 were waited for; matrix products, arithmetic and copies ran while one was open for 10% of the time, Pallas kernels for 0%

profile of v1, /device:TPU:1, one launch (start us, length us, event | category | flops | bytes accessed | tf_op | source)
XLA Modules:
  0.0 417.9 jit_solution(4791345972451215527)
XLA Ops:
  6.5 1.5 copy.40
  8.1 1.2 constant_dynamic-slice_fusion.1
  11.3 0.8 constant_dynamic-slice_fusion
  15.3 7.4 %reshape_squeeze.19 = bf16[2,8192,128]{2,1,0:T(8,128)(2,1)} reshape(bf16[2,1,64,16384]{3,2,1,0:T(8,128)(2,1)} %param.7) | data formatting | bytes 8388608 | tf_op jit(solution)/shard_map/reshape;squeeze | solution.py:36
  22.7 34.6 %all-gather.2.cloned.1.call-done = bf16[2,1,2,512,512]{4,2,1,0,3:T(2,128)(2,1)} async-done(((bf16[2,1,2,16,512]{4,2,1,0,3:T(2,128)(2,1)}), bf16[2,1,2,512,512]{4,2,1,0,3:T(2,128)(2,1)}) %all-gather.2.cloned.1.call-update) | async-done | bytes 2097168 | tf_op jit(solution)/shard_map/all_gather | solution.py:20
  57.3 6.6 %fusion.58 = (bf16[2,1,1,512,512]{4,2,1,0,3:T(2,128)(2,1)}, bf16[2,1,1,512,512]{4,2,1,0,3:T(2,128)(2,1)S(1)}) fusion(bf16[2,1,2,512,512]{4,2,1,0,3:T(2,128)(2,1)} %all-gather.2.cloned.1.call-done), kind=kLoop, calls=%fused_computation.114 | loop fusion | bytes 4194304 | tf_op jit(solution)/shard_map/slice | solution.py:62
  63.9 4.6 %copy.59 = bf16[2,1,1,512,512]{3,4,2,1,0:T(8,128)(2,1)S(1)} copy(bf16[2,1,1,512,512]{4,2,1,0,3:T(2,128)(2,1)} %get-tuple-element.24) | data formatting | bytes 2097152
  68.5 4.2 %copy.60 = bf16[2,1,1,512,512]{3,4,2,1,0:T(8,128)(2,1)} copy(bf16[2,1,1,512,512]{4,2,1,0,3:T(2,128)(2,1)S(1)} %get-tuple-element.25) | data formatting | bytes 2097152
  74.3 3.5 fusion.15
  77.8 1.2 copy.61
  79.0 7.5 %fusion.2 = bf16[64,256,128]{2,1,0:T(8,128)(2,1)} fusion(bf16[64,128,2,128]{1,0,3,2:T(8,128)(2,1)S(1)} %bitcast.220, bf16[1,128,256]{1,2,0:T(8,128)(2,1)S(1)} %get-tuple-element.35, bf16[1,128,256]{1,2,0:T(8,128)(2,1)S(1)} %get-tuple-element.34), kind=kOutput, calls=%fused_computation.12 | convolution fusion | flops 1076101120 | bytes 8519680 | tf_op jit(solution)/shard_map/ijck,cjb->ibk/dot_general | solution.py:39
  86.5 6.9 %reshape.75 = bf16[64,2,16384]{2,1,0:T(2,128)(2,1)} reshape(bf16[64,256,128]{2,1,0:T(8,128)(2,1)} %fusion.2) | data formatting | bytes 8388608 | tf_op jit(solution)/shard_map/reshape | solution.py:40
  93.4 6.7 %copy.85 = bf16[64,2,16384]{2,0,1:T(8,128)(2,1)} copy(bf16[64,2,16384]{2,1,0:T(2,128)(2,1)} %reshape.75) | data formatting | bytes 8388608 | tf_op jit(solution)/shard_map/reshape | solution.py:40
  100.1 1.3 fusion.14
  101.4 1.2 copy.62
  102.6 7.4 %fusion.3 = bf16[64,256,128]{2,1,0:T(8,128)(2,1)} fusion(bf16[64,128,2,128]{1,0,3,2:T(8,128)(2,1)S(1)} %bitcast.221, bf16[1,128,256]{1,2,0:T(8,128)(2,1)S(1)} %get-tuple-element.39, bf16[1,128,256]{1,2,0:T(8,128)(2,1)S(1)} %get-tuple-element.38), kind=kOutput, calls=%fused_computation.13 | convolution fusion | flops 1076101120 | bytes 8519680 | tf_op jit(solution)/shard_map/ijck,cjb->ibk/dot_general | solution.py:39
  110.0 6.9 %reshape.77 = bf16[64,2,16384]{2,1,0:T(2,128)(2,1)} reshape(bf16[64,256,128]{2,1,0:T(8,128)(2,1)} %fusion.3) | data formatting | bytes 8388608 | tf_op jit(solution)/shard_map/reshape | solution.py:40
  116.9 6.6 %copy.84 = bf16[64,2,16384]{2,0,1:T(8,128)(2,1)} copy(bf16[64,2,16384]{2,1,0:T(2,128)(2,1)} %reshape.77) | data formatting | bytes 8388608 | tf_op jit(solution)/shard_map/reshape | solution.py:40
  123.5 6.2 %pad_maximum_fusion = bf16[2,2,64,16384]{3,2,1,0:T(8,128)(2,1)} fusion(bf16[2,1,64,16384]{3,2,1,0:T(8,128)(2,1)} %bitcast.224, bf16[2,1,64,16384]{3,2,1,0:T(8,128)(2,1)S(1)} %bitcast.222), kind=kLoop, calls=%fused_computation.9 | loop fusion | flops 4194304 | bytes 16777216 | tf_op jit(solution)/shard_map/stack | solution.py:48
  129.7 34.5 %copy.49 = bf16[2,2,64,16384]{2,1,0,3:T(2,128)(2,1)} copy(bf16[2,2,64,16384]{3,2,1,0:T(8,128)(2,1)} %pad_maximum_fusion) | data formatting | bytes 16777216 | tf_op jit(solution)/shard_map/stack | solution.py:48
  164.2 26.7 %reshape.124 = bf16[32,2,65536]{2,1,0:T(2,128)(2,1)} reshape(bf16[16384,2,2,64]{3,2,1,0:T(2,128)(2,1)} %bitcast.213) | data formatting | bytes 16777216
  190.9 5.4 %all-to-all-start = ((bf16[32,2,65536]{2,1,0:T(2,128)(2,1)}), bf16[32,2,65536]{2,1,0:T(2,128)(2,1)}, u32[]{:S(2)}, u32[]{:S(2)}) async-start(bf16[32,2,65536]{2,1,0:T(2,128)(2,1)} %reshape.124), calls=%async_computation | async-start | bytes 16777216 | tf_op jit(solution)/shard_map/all_to_all | solution.py:49
  196.4 5.8 %fusion.57 = (bf16[2,1,2048,512]{3,2,1,0:T(8,128)(2,1)}, bf16[2,1,2048,512]{3,2,1,0:T(8,128)(2,1)}) fusion(bf16[2,2,2048,512]{3,2,1,0:T(8,128)(2,1)} %param.8), kind=kLoop, calls=%fused_computation.113 | loop fusion | bytes 16777216 | tf_op jit(solution)/shard_map/slice | solution.py:53
  202.2 4.9 %gather_fusion.3 = bf16[16,2,128,512]{3,2,1,0:T(8,128)(2,1)} fusion(bf16[2,16,128,512]{3,2,1,0:T(8,128)(2,1)} %bitcast.225, s32[1024]{0:T(1024)S(1)} %pad_clamp_fusion), kind=kCustom, calls=%fused_computation.clone | custom fusion | bytes 8388672 | tf_op jit(solution)/shard_map/jit(_take)/gather | solution.py:54
  207.1 5.0 %gather_fusion.4 = bf16[16,2,128,512]{3,2,1,0:T(8,128)(2,1)} fusion(bf16[2,16,128,512]{3,2,1,0:T(8,128)(2,1)} %bitcast.223, s32[1024]{0:T(1024)S(1)} %pad_clamp_fusion), kind=kCustom, calls=%fused_computation.1.clone | custom fusion | bytes 8388672 | tf_op jit(solution)/shard_map/jit(_take)/gather | solution.py:54
  212.9 6.1 %fusion.5 = (bf16[2,16,128,512]{3,2,1,0:T(8,128)(2,1)}, bf16[2,16,128,512]{3,2,1,0:T(8,128)(2,1)}) fusion(bf16[16,2,128,512]{3,2,1,0:T(8,128)(2,1)} %gather_fusion.3, pred[16]{0:T(512)(128)(4,1)S(1)} %compare_and_fusion, bf16[16,2,128,512]{3,2,1,0:T(8,128)(2,1)} %gather_fusion.4), kind=kLoop, calls=%fused_computation.17 | loop fusion | flops 4194304 | bytes 16777232 | tf_op jit(solution)/shard_map/jit(_take)/select_n | solution.py:54
  219.2 1.1 reshape_squeeze.21
  220.4 1.4 copy.42
  221.8 1.7 copy.52
  223.6 2.0 gather_fusion.1
  226.3 1.6 copy_convert_fusion.1
  227.8 1.6 copy_convert_fusion
  229.4 74.0 %all-to-all-done = bf16[32,2,65536]{2,1,0:T(2,128)(2,1)} async-done(((bf16[32,2,65536]{2,1,0:T(2,128)(2,1)}), bf16[32,2,65536]{2,1,0:T(2,128)(2,1)}, u32[]{:S(2)}, u32[]{:S(2)}) %all-to-all-start) | async-done | bytes 8388640 | tf_op jit(solution)/shard_map/all_to_all | solution.py:49
  303.5 26.0 %reshape.125 = bf16[16384,2,2,64]{3,2,1,0:T(2,128)(2,1)} reshape(bf16[32,2,65536]{2,1,0:T(2,128)(2,1)} %all-to-all-done) | data formatting | bytes 16777216
  329.5 36.0 %copy.50 = bf16[2,2,32,64,512]{4,3,2,1,0:T(8,128)(2,1)} copy(bf16[2,2,32,64,512]{3,1,0,4,2:T(2,128)(2,1)} %bitcast.214) | data formatting | bytes 16777216 | tf_op jit(solution)/shard_map/all_to_all | solution.py:49
  365.5 4.0 fusion.56
  372.3 1.4 copy-done.2
  375.9 0.9 copy-done.7
  376.8 0.8 subtract_reduce_fusion.1
  378.4 0.8 subtract_reduce_fusion
  379.2 7.1 %collective-permute-start = (f32[2,1,2,16,1]{3,2,0,4,1:T(2,128)S(1)}, f32[2,1,2,16,1]{3,2,0,4,1:T(2,128)S(1)}, u32[]{:S(2)}, u32[]{:S(2)}) collective-permute-start(f32[2,1,2,16,1]{3,2,0,4,1:T(2,128)S(1)} %bitcast.232), channel_id=1, source_target_pairs={{0,1},{1,0},{2,3},{3,2},{4,5},{5,4},{6,7},{7,6},{8,9},{9,8},{10,11... | collective-permute-start | bytes 776 | tf_op jit(solution)/shard_map/ppermute | solution.py:80
  386.3 0.8 collective-permute-done
  387.1 12.0 %collective-permute-start.1 = (f32[2,1,2,16,1]{3,2,0,4,1:T(2,128)S(1)}, f32[2,1,2,16,1]{3,2,0,4,1:T(2,128)S(1)}, u32[]{:S(2)}, u32[]{:S(2)}) collective-permute-start(f32[2,1,2,16,1]{3,2,0,4,1:T(2,128)S(1)} %fusion.51), channel_id=1, source_target_pairs={{0,2},{1,3},{2,0},{3,1},{4,6},{5,7},{6,4},{7,5},{8,10},{9,11},{10,... | collective-permute-start | bytes 776 | tf_op jit(solution)/shard_map/ppermute | solution.py:80
  399.1 1.0 collective-permute-done.1
  400.1 3.9 collective-permute-done.2
  404.0 2.4 collective-permute-done.3
  406.5 2.5 collective-permute-start.4
  409.0 1.4 collective-permute-done.4
  (52 shorter events, 10.4 us)
Async XLA Ops:
  6.5 50.8 %all-gather.2.cloned.1.call-start = ((), (), s32[]{:S(2)}) async-start(), calls=%async_computation.1 | async-start | bytes 2162688 | tf_op jit(solution)/shard_map/all_gather | solution.py:20
  93.4 6.7 %copy-start.1 = (bf16[2,8192,128]{2,1,0:T(8,128)(2,1)S(1)}, bf16[2,8192,128]{2,1,0:T(8,128)(2,1)}, u32[]{:S(2)}) copy-start(bf16[2,8192,128]{2,1,0:T(8,128)(2,1)} %reshape_squeeze.19) | copy-start | bytes 12582916
  116.9 6.6 %copy-start.4 = (bf16[64,2,16384]{2,0,1:T(8,128)(2,1)S(1)}, bf16[64,2,16384]{2,0,1:T(8,128)(2,1)}, u32[]{:S(2)}) copy-start(bf16[64,2,16384]{2,0,1:T(8,128)(2,1)} %copy.85) | copy-start | bytes 12582916
  190.9 5.4 %copy-start.8 = (s32[16,1]{0,1:T(1,128)S(1)}, s32[16,1]{0,1:T(1,128)}, u32[]{:S(2)}) copy-start(s32[16,1]{0,1:T(1,128)} %param.10) | copy-start | bytes 196
  190.9 112.6 %all-to-all-start = ((bf16[32,2,65536]{2,1,0:T(2,128)(2,1)}), bf16[32,2,65536]{2,1,0:T(2,128)(2,1)}, u32[]{:S(2)}, u32[]{:S(2)}) async-start(bf16[32,2,65536]{2,1,0:T(2,128)(2,1)} %reshape.124), calls=%async_computation | async-start | bytes 16777216 | tf_op jit(solution)/shard_map/all_to_all | solution.py:49
  207.1 5.0 %copy-start = (s32[16,3]{0,1:T(4,128)S(1)}, s32[16,3]{0,1:T(4,128)}, u32[]{:S(2)}) copy-start(s32[16,3]{0,1:T(4,128)} %param.11) | copy-start | bytes 580
  212.8 6.4 %copy-start.5 = (bf16[2,1,1,512,512]{3,4,2,1,0:T(8,128)(2,1)S(1)}, bf16[2,1,1,512,512]{3,4,2,1,0:T(8,128)(2,1)}, u32[]{:S(2)}) copy-start(bf16[2,1,1,512,512]{3,4,2,1,0:T(8,128)(2,1)} %copy.60) | copy-start | bytes 3145732
  365.5 4.7 %copy-start.3 = (bf16[2,16,128,512]{3,2,1,0:T(8,128)(2,1)S(1)}, bf16[2,16,128,512]{3,2,1,0:T(8,128)(2,1)}, u32[]{:S(2)}) copy-start(bf16[2,16,128,512]{3,2,1,0:T(8,128)(2,1)} %get-tuple-element.48) | copy-start | bytes 12582916
  371.6 2.2 copy-start.2
  375.2 1.6 copy-start.7
  376.8 1.6 copy-start.6
  379.2 7.9 %collective-permute-start = (f32[2,1,2,16,1]{3,2,0,4,1:T(2,128)S(1)}, f32[2,1,2,16,1]{3,2,0,4,1:T(2,128)S(1)}, u32[]{:S(2)}, u32[]{:S(2)}) collective-permute-start(f32[2,1,2,16,1]{3,2,0,4,1:T(2,128)S(1)} %bitcast.232), channel_id=1, source_target_pairs={{0,1},{1,0},{2,3},{3,2},{4,5},{5,4},{6,7},{7,6},{8,9},{9,8},{10,11... | collective-permute-start | bytes 776 | tf_op jit(solution)/shard_map/ppermute | solution.py:80
  387.1 13.0 %collective-permute-start.1 = (f32[2,1,2,16,1]{3,2,0,4,1:T(2,128)S(1)}, f32[2,1,2,16,1]{3,2,0,4,1:T(2,128)S(1)}, u32[]{:S(2)}, u32[]{:S(2)}) collective-permute-start(f32[2,1,2,16,1]{3,2,0,4,1:T(2,128)S(1)} %fusion.51), channel_id=1, source_target_pairs={{0,2},{1,3},{2,0},{3,1},{4,6},{5,7},{6,4},{7,5},{8,10},{9,11},{10,... | collective-permute-start | bytes 776 | tf_op jit(solution)/shard_map/ppermute | solution.py:80
  400.1 3.9 collective-permute-start.2
  404.0 2.4 collective-permute-start.3
  406.5 3.9 collective-permute-start.4
Sparse Core Ops, SparseCore 0:
  9.6 47.6 all-gather.1
